TPU v7x, 32 devices: a whole 2x2x4 slice. The times are simulated.
32 devices in a mesh: fsdp: 8 (over y, x, core), ep: 4 (over z).
Axes of the slice: x: 2, y: 2, z: 4, core: 2. Of those that a mesh axis runs over, the one named last changes fastest.
Arguments:
- hidden: bfloat16 [2048, 8192], P('fsdp', 'ep'), may hold values from -6 to 6
- w_down: bfloat16 [6144, 2, 8192], P('fsdp', None, 'ep'), may hold values from -0.0625 to 0.0625
- route_ids: int32 [1024, 2], P('fsdp'), may hold values from 0 to 7, as said below
- probs: float32 [1024, 2], P('fsdp'), may hold values from 0.1 to 0.9
- grad_out: bfloat16 [1024, 6144], P('fsdp', 'ep'), may hold values from -6 to 6
Outputs:
- output: bfloat16 [1024, 6144], P('fsdp', 'ep')
- grad_hidden: bfloat16 [2048, 8192], P('fsdp', 'ep')
- grad_weight: bfloat16 [6144, 2, 8192], P('fsdp', None, 'ep')
- grad_probs: float32 [1024, 2], P('fsdp')
Inputs may be any that keep to these rules, and one draw needn't show every extreme that they name: `route_ids`: each token names 2 different experts. Within one panel's 128 tokens, experts 0 and 1 are each named by 1 to 128 tokens, and in some panel both are named by all 128 tokens.
All inputs are finite; a program needn't handle non-finite values.
Results may differ from a plain program's by a relative error of at most 0.012.
Values may be sent and summed in bfloat16 or wider, within the bound.
A program may use at most 384 MiB of HBM per device.

v0:
```python
import jax
import jax.numpy as jnp
from jax import lax
from jax.sharding import PartitionSpec as P

BLOCK = 128


def route_layout(route_part, prob_part, expert_count, block_rows, row_count):
    token_count = route_part.shape[0]
    experts = jnp.arange(expert_count, dtype=jnp.int32)
    hits = (route_part[:, :, None] == experts[None, None, :]).astype(jnp.int32)
    named = jnp.sum(hits, axis=1)
    counts = jnp.sum(named, axis=0)
    ranks = jnp.cumsum(named, axis=0) - named
    padded = (counts + block_rows - 1) // block_rows * block_rows
    offsets = jnp.cumsum(padded) - padded
    row_of = jnp.sum(hits * (offsets[None, None, :] + ranks[:, None, :]), axis=2)
    valid = jnp.sum(hits, axis=2)
    starts = jnp.arange(row_count // block_rows, dtype=jnp.int32) * block_rows
    inside = (starts[:, None] >= offsets[None, :]) & (starts[:, None] < (offsets + padded)[None, :])
    block_exp = jnp.sum(jnp.where(inside, experts[None, :] + 1, 0), axis=1) - 1
    target = jnp.where(valid > 0, row_of, row_count).reshape(-1)
    token_index = jnp.broadcast_to(
        jnp.arange(token_count, dtype=jnp.int32)[:, None], route_part.shape
    ).reshape(-1)
    row_tok = jnp.zeros((row_count,), jnp.int32).at[target].set(token_index, mode="drop")
    row_live = (
        jnp.zeros((row_count,), jnp.int32).at[target].set(jnp.ones_like(token_index), mode="drop")
    )
    row_prob = (
        jnp.zeros((row_count,), prob_part.dtype).at[target].set(prob_part.reshape(-1), mode="drop")
    )
    return (row_of, valid, block_exp, row_tok, row_live, row_prob)


def local(hidden, w_down, route_ids, probs, grad_out):
    row_count, unit_count = hidden.shape
    expert_count = w_down.shape[1]
    block_count = row_count // BLOCK
    row_of, valid, block_exp, row_tok, row_live, row_prob = route_layout(
        route_ids, probs, expert_count, BLOCK, row_count
    )
    safe_exp = jnp.maximum(block_exp, 0)
    prob_valid = probs * valid.astype(jnp.float32)
    full_grads = lax.all_gather(grad_out, "ep", axis=1, tiled=True)
    model_width = full_grads.shape[1]
    routed = jnp.where(row_live[:, None] > 0, full_grads[row_tok], jnp.zeros((), jnp.bfloat16))
    scaled = (row_prob[:, None] * routed.astype(jnp.float32)).astype(jnp.bfloat16)
    hid_blocks = hidden.reshape(block_count, BLOCK, unit_count)
    routed_blocks = routed.reshape(block_count, BLOCK, model_width)
    row_exp = jnp.repeat(block_exp, BLOCK)
    member = (row_exp[:, None] == jnp.arange(expert_count, dtype=jnp.int32)[None, :]).astype(
        jnp.bfloat16
    )
    masked_hid = hidden[:, None, :] * member[:, :, None]
    piece = lax.all_gather(w_down, "fsdp", axis=0, tiled=True)
    width = piece.shape[0]
    chosen = jnp.take(piece, safe_exp, axis=1)
    out_rows = jnp.einsum(
        "bri,dbi->brd", hid_blocks, chosen, preferred_element_type=jnp.float32
    ).reshape(row_count, width)
    back_total = jnp.einsum(
        "brd,dbi->bri", routed_blocks, chosen, preferred_element_type=jnp.float32
    )
    combined = jnp.sum(prob_valid[:, :, None] * out_rows[row_of], axis=1)
    out_total = combined
    out_total, back_total = (out_total, back_total)
    grad_weight = lax.psum_scatter(
        jnp.einsum("rd,rei->dei", scaled, masked_hid, preferred_element_type=jnp.float32).astype(
            jnp.bfloat16
        ),
        "fsdp",
        scatter_dimension=0,
        tiled=True,
    )
    output = lax.psum_scatter(out_total.astype(jnp.bfloat16), "ep", scatter_dimension=1, tiled=True)
    hidden_back = back_total.reshape(row_count, unit_count)
    grad_hidden = (row_prob[:, None] * hidden_back).astype(jnp.bfloat16)
    row_dot = jnp.sum(hidden.astype(jnp.float32) * hidden_back, axis=1)
    prob_terms = valid.astype(jnp.float32) * row_dot[row_of]
    grad_probs = lax.psum(prob_terms, "ep")
    return (output, grad_hidden, grad_weight, grad_probs)


def solution(mesh):
    placed = (
        P("fsdp", "ep"),
        P("fsdp", None, "ep"),
        P("fsdp", None),
        P("fsdp", None),
        P("fsdp", "ep"),
    )
    return jax.shard_map(
        local,
        mesh=mesh,
        in_specs=placed,
        out_specs=(P("fsdp", "ep"), P("fsdp", "ep"), P("fsdp", None, "ep"), P("fsdp", None)),
        check_vma=False,
    )
```

profile of v0, /device:TPU:0, one launch (start us, length us, event | category | flops | bytes accessed | tf_op | source)
XLA Modules:
  0.0 635.5 jit_solution(14992355778642910269)
XLA Ops:
  7.9 8.4 %copy.21 = bf16[768,2,2048]{2,0,1:T(8,128)(2,1)} copy(bf16[768,2,2048]{2,1,0:T(2,128)(2,1)} %param.6) | data formatting | bytes 12582912 | tf_op args[1]
  23.5 25.9 %all-gather.5.cloned.1.call-done = bf16[128,6144]{1,0:T(8,128)(2,1)} async-done(((bf16[128,1536]{1,0:T(8,128)(2,1)}), bf16[128,6144]{1,0:T(8,128)(2,1)}) %all-gather.5.cloned.1.call-update) | async-done | bytes 1572880 | tf_op jit(solution)/shard_map/all_gather | solution.py:46
  49.4 7.1 %gather_fusion.1 = bf16[256,6144]{1,0:T(8,128)(2,1)S(1)} fusion(bf16[128,6144]{1,0:T(8,128)(2,1)} %all-gather.5.cloned.1.call-done, s32[1024]{0:T(1024)S(1)} %pad_clamp_fusion), kind=kCustom, calls=%fused_computation.1 | custom fusion | bytes 6292480 | tf_op jit(solution)/shard_map/gather | solution.py:48
  56.5 24.9 %convolution_convert_fusion = bf16[6144,2,2048]{2,0,1:T(8,128)(2,1)} fusion(bf16[256,6144]{1,0:T(8,128)(2,1)S(1)} %gather_fusion.1, f32[256]{0:T(256)S(1)} %scatter_custom_fusion, pred[256]{0:T(512)(128)(4,1)S(1)} %broadcast_compare_fusion, bf16[256,2]{0,1:T(2,128)(2,1)S(1)} %compare_convert_fusion, bf16[256,2048]{1,0:T(8,128)(2,1)} %param.5), kind=kOutput, calls=%fused_computation.31 | convolution fusion | flops 12920553472 | bytes 54528256 | tf_op jit(solution)/shard_map/rd,rei->dei/dot_general | solution.py:70
  83.2 199.5 %all-gather.3.cloned.1.call-done = bf16[6144,2,2048]{2,0,1:T(8,128)(2,1)} async-done(((bf16[768,2,2048]{2,0,1:T(8,128)(2,1)}), bf16[6144,2,2048]{2,0,1:T(8,128)(2,1)}) %all-gather.3.cloned.1.call-update) | async-done | bytes 50331664 | tf_op jit(solution)/shard_map/all_gather | solution.py:57
  282.7 41.5 %fusion.28 = (bf16[512,2,2048]{2,0,1:T(8,128)(2,1)}, bf16[512,2,2048]{2,0,1:T(8,128)(2,1)}, bf16[512,2,2048]{2,0,1:T(8,128)(2,1)}, bf16[512,2,2048]{2,0,1:T(8,12...) fusion(bf16[6144,2,2048]{2,0,1:T(8,128)(2,1)} %all-gather.3.clo, ...), kind=kLoop, calls=%fused_computation.108 | loop fusion | bytes 100663296 | tf_op jit(solution)/shard_map/jit(_take)/gather | solution.py:59
  327.2 9.6 %while.12 = (s32[]{:T(128)}, bf16[512,2,2048]{2,0,1:T(8,128)(2,1)}, s32[2,1]{0,1:T(1,128)S(1)}, bf16[2,512,2048]{2,1,0:T(8,128)(2,1)}, s32[]{:T(128)}) while((s32[]{:T(128)}, bf16[512,2,2048]{2,0,1:T(8,128)(2,1)}, s32[2,1]{0,1:T(1,128)S(1)}, bf16[2,512,2048]{2,1,0:T(8,128)(2,1)}, s32[]{:T(128)}) %tuple.161), condition=%wide.while_cond, body=%wide.while_body.sunk | while | flops 2 | bytes 4195401 | solution.py:59
  327.8 4.2 bitcast_dynamic-update-slice_fusion.36
  332.5 4.3 bitcast_dynamic-update-slice_fusion.36
  339.9 9.5 %while.13 = (s32[]{:T(128)}, bf16[512,2,2048]{2,0,1:T(8,128)(2,1)}, s32[2,1]{0,1:T(1,128)S(1)}, bf16[2,512,2048]{2,1,0:T(8,128)(2,1)}, s32[]{:T(128)}) while((s32[]{:T(128)}, bf16[512,2,2048]{2,0,1:T(8,128)(2,1)}, s32[2,1]{0,1:T(1,128)S(1)}, bf16[2,512,2048]{2,1,0:T(8,128)(2,1)}, s32[]{:T(128)}) %tuple.205), condition=%wide.while_cond.1, body=%wide.while_body.1.sunk | while | flops 2 | bytes 4195401 | solution.py:59
  340.5 4.3 bitcast_dynamic-update-slice_fusion.37
  345.4 4.0 bitcast_dynamic-update-slice_fusion.37
  352.0 8.8 %while.14 = (s32[]{:T(128)}, bf16[512,2,2048]{2,0,1:T(8,128)(2,1)}, s32[2,1]{0,1:T(1,128)S(1)}, bf16[2,512,2048]{2,1,0:T(8,128)(2,1)}, s32[]{:T(128)}) while((s32[]{:T(128)}, bf16[512,2,2048]{2,0,1:T(8,128)(2,1)}, s32[2,1]{0,1:T(1,128)S(1)}, bf16[2,512,2048]{2,1,0:T(8,128)(2,1)}, s32[]{:T(128)}) %tuple.206), condition=%wide.while_cond.2, body=%wide.while_body.2.sunk | while | flops 2 | bytes 4195401 | solution.py:59
  352.5 3.8 bitcast_dynamic-update-slice_fusion.38
  356.9 3.9 bitcast_dynamic-update-slice_fusion.38
  363.4 9.2 %while.15 = (s32[]{:T(128)}, bf16[512,2,2048]{2,0,1:T(8,128)(2,1)}, s32[2,1]{0,1:T(1,128)S(1)}, bf16[2,512,2048]{2,1,0:T(8,128)(2,1)}, s32[]{:T(128)}) while((s32[]{:T(128)}, bf16[512,2,2048]{2,0,1:T(8,128)(2,1)}, s32[2,1]{0,1:T(1,128)S(1)}, bf16[2,512,2048]{2,1,0:T(8,128)(2,1)}, s32[]{:T(128)}) %tuple.207), condition=%wide.while_cond.3, body=%wide.while_body.3.sunk | while | flops 2 | bytes 4195401 | solution.py:59
  363.9 4.1 bitcast_dynamic-update-slice_fusion.39
  368.6 3.9 bitcast_dynamic-update-slice_fusion.39
  375.1 9.1 %while.16 = (s32[]{:T(128)}, bf16[512,2,2048]{2,0,1:T(8,128)(2,1)}, s32[2,1]{0,1:T(1,128)S(1)}, bf16[2,512,2048]{2,1,0:T(8,128)(2,1)}, s32[]{:T(128)}) while((s32[]{:T(128)}, bf16[512,2,2048]{2,0,1:T(8,128)(2,1)}, s32[2,1]{0,1:T(1,128)S(1)}, bf16[2,512,2048]{2,1,0:T(8,128)(2,1)}, s32[]{:T(128)}) %tuple.208), condition=%wide.while_cond.4, body=%wide.while_body.4.sunk | while | flops 2 | bytes 4195401 | solution.py:59
  375.7 3.9 bitcast_dynamic-update-slice_fusion.40
  380.1 4.1 bitcast_dynamic-update-slice_fusion.40
  386.7 8.8 %while.17 = (s32[]{:T(128)}, bf16[512,2,2048]{2,0,1:T(8,128)(2,1)}, s32[2,1]{0,1:T(1,128)S(1)}, bf16[2,512,2048]{2,1,0:T(8,128)(2,1)}, s32[]{:T(128)}) while((s32[]{:T(128)}, bf16[512,2,2048]{2,0,1:T(8,128)(2,1)}, s32[2,1]{0,1:T(1,128)S(1)}, bf16[2,512,2048]{2,1,0:T(8,128)(2,1)}, s32[]{:T(128)}) %tuple.209), condition=%wide.while_cond.5, body=%wide.while_body.5.sunk | while | flops 2 | bytes 4195401 | solution.py:59
  391.6 3.8 bitcast_dynamic-update-slice_fusion.41
  398.1 8.8 %while.18 = (s32[]{:T(128)}, bf16[512,2,2048]{2,0,1:T(8,128)(2,1)}, s32[2,1]{0,1:T(1,128)S(1)}, bf16[2,512,2048]{2,1,0:T(8,128)(2,1)}, s32[]{:T(128)}) while((s32[]{:T(128)}, bf16[512,2,2048]{2,0,1:T(8,128)(2,1)}, s32[2,1]{0,1:T(1,128)S(1)}, bf16[2,512,2048]{2,1,0:T(8,128)(2,1)}, s32[]{:T(128)}) %tuple.210), condition=%wide.while_cond.6, body=%wide.while_body.6.sunk | while | flops 2 | bytes 4195401 | solution.py:59
  398.6 3.8 bitcast_dynamic-update-slice_fusion.42
  403.0 3.9 bitcast_dynamic-update-slice_fusion.42
  409.4 9.3 %while.19 = (s32[]{:T(128)}, bf16[512,2,2048]{2,0,1:T(8,128)(2,1)}, s32[2,1]{0,1:T(1,128)S(1)}, bf16[2,512,2048]{2,1,0:T(8,128)(2,1)}, s32[]{:T(128)}) while((s32[]{:T(128)}, bf16[512,2,2048]{2,0,1:T(8,128)(2,1)}, s32[2,1]{0,1:T(1,128)S(1)}, bf16[2,512,2048]{2,1,0:T(8,128)(2,1)}, s32[]{:T(128)}) %tuple.211), condition=%wide.while_cond.7, body=%wide.while_body.7.sunk | while | flops 2 | bytes 4195401 | solution.py:59
  410.0 4.2 bitcast_dynamic-update-slice_fusion.43
  414.8 4.0 bitcast_dynamic-update-slice_fusion.43
  421.2 8.8 %while.20 = (s32[]{:T(128)}, bf16[512,2,2048]{2,0,1:T(8,128)(2,1)}, s32[2,1]{0,1:T(1,128)S(1)}, bf16[2,512,2048]{2,1,0:T(8,128)(2,1)}, s32[]{:T(128)}) while((s32[]{:T(128)}, bf16[512,2,2048]{2,0,1:T(8,128)(2,1)}, s32[2,1]{0,1:T(1,128)S(1)}, bf16[2,512,2048]{2,1,0:T(8,128)(2,1)}, s32[]{:T(128)}) %tuple.212), condition=%wide.while_cond.8, body=%wide.while_body.8.sunk | while | flops 2 | bytes 4195401 | solution.py:59
  421.8 3.8 bitcast_dynamic-update-slice_fusion.44
  426.2 3.9 bitcast_dynamic-update-slice_fusion.44
  432.5 8.7 %while.21 = (s32[]{:T(128)}, bf16[512,2,2048]{2,0,1:T(8,128)(2,1)}, s32[2,1]{0,1:T(1,128)S(1)}, bf16[2,512,2048]{2,1,0:T(8,128)(2,1)}, s32[]{:T(128)}) while((s32[]{:T(128)}, bf16[512,2,2048]{2,0,1:T(8,128)(2,1)}, s32[2,1]{0,1:T(1,128)S(1)}, bf16[2,512,2048]{2,1,0:T(8,128)(2,1)}, s32[]{:T(128)}) %tuple.213), condition=%wide.while_cond.9, body=%wide.while_body.9.sunk | while | flops 2 | bytes 4195401 | solution.py:59
  443.9 8.9 %while.22 = (s32[]{:T(128)}, bf16[512,2,2048]{2,0,1:T(8,128)(2,1)}, s32[2,1]{0,1:T(1,128)S(1)}, bf16[2,512,2048]{2,1,0:T(8,128)(2,1)}, s32[]{:T(128)}) while((s32[]{:T(128)}, bf16[512,2,2048]{2,0,1:T(8,128)(2,1)}, s32[2,1]{0,1:T(1,128)S(1)}, bf16[2,512,2048]{2,1,0:T(8,128)(2,1)}, s32[]{:T(128)}) %tuple.214), condition=%wide.while_cond.10, body=%wide.while_body.10.sunk | while | flops 2 | bytes 4195401 | solution.py:59
  444.5 3.9 bitcast_dynamic-update-slice_fusion.46
  448.9 3.9 bitcast_dynamic-update-slice_fusion.46
  455.3 9.4 %while.23 = (s32[]{:T(128)}, bf16[512,2,2048]{2,0,1:T(8,128)(2,1)}, s32[2,1]{0,1:T(1,128)S(1)}, bf16[2,512,2048]{2,1,0:T(8,128)(2,1)}, s32[]{:T(128)}) while((s32[]{:T(128)}, bf16[512,2,2048]{2,0,1:T(8,128)(2,1)}, s32[2,1]{0,1:T(1,128)S(1)}, bf16[2,512,2048]{2,1,0:T(8,128)(2,1)}, s32[]{:T(128)}) %tuple.215), condition=%wide.while_cond.11, body=%wide.while_body.11.sunk | while | flops 2 | bytes 4195401 | solution.py:59
  455.9 4.1 bitcast_dynamic-update-slice_fusion.47
  460.6 4.2 bitcast_dynamic-update-slice_fusion.47
  464.7 5.3 bitcast_dynamic-update-slice_fusion.23
  510.1 25.9 %fusion.1 = f32[2,6144,128]{1,2,0:T(8,128)} fusion(bf16[2,128,2048]{2,1,0:T(8,128)(2,1)S(1)} %bitcast.149, bf16[6144,2,2048]{2,0,1:T(8,128)(2,1)} %bitcast_dynamic-update-slice_fusion.12, pred[2]{0:T(512)(128)(4,1)S(1)} %maximum_compare_fusion), kind=kOutput, calls=%fused_computation.33 | convolution fusion | flops 6467616768 | bytes 57671680 | tf_op jit(solution)/shard_map/bri,dbi->brd/dot_general | solution.py:60
  536.0 10.6 %gather_fusion = f32[256,6144]{1,0:T(8,128)} fusion(f32[256,6144]{1,0:T(8,128)} %bitcast.147, s32[1024]{0:T(1024)S(1)} %copy-done.14), kind=kCustom, calls=%fused_computation | custom fusion | bytes 12583936 | tf_op jit(solution)/shard_map/gather | solution.py:66
  546.6 8.4 %reshape.505 = f32[128,2,6144]{2,1,0:T(2,128)} reshape(f32[256,6144]{1,0:T(8,128)} %gather_fusion) | data formatting | bytes 12582912 | tf_op jit(solution)/shard_map/gather | solution.py:66
  555.0 20.2 %fusion = f32[2,128,2048]{2,1,0:T(8,128)} fusion(bf16[6144,2,2048]{2,0,1:T(8,128)(2,1)} %bitcast_dynamic-update-slice_fusion.12, pred[2]{0:T(512)(128)(4,1)S(1)} %maximum_compare_fusion, bf16[2,128,6144]{2,1,0:T(8,128)(2,1)S(1)} %bitcast.148, pred[2,128]{1,0:T(4,128)(4,1)S(1)} %copy-done.22), kind=kOutput, calls=%fused_computation.32 | convolution fusion | flops 6469189632 | bytes 55574784 | tf_op jit(solution)/shard_map/brd,dbi->bri/dot_general | solution.py:63
  581.0 11.9 %multiply_reduce_fusion = bf16[128,6144]{1,0:T(8,128)(2,1)} fusion(f32[128,2,6144]{2,1,0:T(2,128)} %reshape.505, f32[128,2]{1,0:T(8,128)S(1)} %copy.20), kind=kLoop, calls=%fused_computation.35 | loop fusion | flops 2359296 | bytes 7865344 | tf_op jit(solution)/shard_map/reduce_sum | solution.py:66
  592.9 12.6 %copy.30 = bf16[768,2,2048]{2,1,0:T(2,128)(2,1)} copy(bf16[768,2,2048]{2,0,1:T(8,128)(2,1)} %reduce-scatter.5.cloned.1.call-done) | data formatting | bytes 12582912
  605.5 12.9 %psum.7 = f32[128,2]{0,1:T(2,128)} all-reduce(f32[128,2]{0,1:T(2,128)S(1)} %get-tuple-element.225), channel_id=1, replica_groups=mesh['fsdp'=8,'ep'=4] {'ep'}, use_global_device_ids=true, to_apply=%region_14.15 | all-reduce | flops 256 | bytes 2048 | tf_op jit(solution)/shard_map/psum | solution.py:82
  618.5 10.2 %reduce-scatter.3.cloned.1.call-done = bf16[128,1536]{1,0:T(8,128)(2,1)} async-done(((bf16[128,6144]{1,0:T(8,128)(2,1)}), bf16[128,1536]{1,0:T(8,128)(2,1)}) %reduce-scatter.3.cloned.1.call-update) | async-done | bytes 393232 | tf_op jit(solution)/shard_map/reduce_scatter | solution.py:77
  (146 shorter events, 112.0 us)
Async XLA Ops:
  7.2 42.2 %all-gather.5.cloned.1.call-start = ((), (), s32[]{:S(2)}) async-start(), calls=%async_computation.4 | async-start | bytes 1966080 | tf_op jit(solution)/shard_map/all_gather | solution.py:46
  7.9 274.8 %all-gather.3.cloned.1.call-start = ((), (), s32[]{:S(2)}) async-start(), calls=%async_computation.2 | async-start | bytes 56623104 | tf_op jit(solution)/shard_map/all_gather | solution.py:57
  16.3 0.7 copy-start.21
  16.3 4.7 copy-start.19
  16.4 576.5 %reduce-scatter.5.cloned.1.call-start = ((), (), s32[]{:S(2)}) async-start(), calls=%async_computation.5 | async-start | bytes 56623104 | tf_op jit(solution)/shard_map/reduce_scatter | solution.py:69
  17.1 6.4 %copy-start.17 = (s32[128,2]{0,1:T(2,128)}, s32[128,2]{0,1:T(2,128)S(1)}, u32[]{:S(2)}) copy-start(s32[128,2]{0,1:T(2,128)S(1)} %get-tuple-element.112) | copy-start | bytes 3076
  23.2 33.3 %copy-start.15 = (f32[256]{0:T(256)}, f32[256]{0:T(256)S(1)}, u32[]{:S(2)}) copy-start(f32[256]{0:T(256)S(1)} %scatter_custom_fusion) | copy-start | bytes 3076
  56.5 25.0 %copy-start.11 = (bf16[256,6144]{1,0:T(8,128)(2,1)}, bf16[256,6144]{1,0:T(8,128)(2,1)S(1)}, u32[]{:S(2)}) copy-start(bf16[256,6144]{1,0:T(8,128)(2,1)S(1)} %gather_fusion.1) | copy-start | bytes 9437188
  81.5 547.2 %reduce-scatter.3.cloned.1.call-start = ((), (), s32[]{:S(2)}) async-start(), calls=%async_computation.3 | async-start | bytes 1966080 | tf_op jit(solution)/shard_map/reduce_scatter | solution.py:77
  464.7 5.3 copy-start.1
  470.0 3.8 copy-start.2
  473.9 3.9 copy-start.3
  477.7 3.9 copy-start.4
  481.6 3.7 copy-start.5
  485.3 3.7 copy-start.6
  489.0 3.7 copy-start.7
  492.8 3.7 copy-start.8
  496.5 3.7 copy-start.9
  500.2 4.0 copy-start.10
  504.2 3.7 copy-start
  507.9 2.2 copy-start.13
  510.1 25.9 %copy-start.14 = (s32[1024]{0:T(1024)S(1)}, s32[1024]{0:T(1024)}, u32[]{:S(2)}) copy-start(s32[1024]{0:T(1024)} %pad_clamp_fusion.1) | copy-start | bytes 12292
  546.6 8.4 %copy-start.12 = (bf16[256,6144]{1,0:T(8,128)(2,1)S(1)}, bf16[256,6144]{1,0:T(8,128)(2,1)}, u32[]{:S(2)}) copy-start(bf16[256,6144]{1,0:T(8,128)(2,1)} %copy-done.11) | copy-start | bytes 9437188
  546.6 8.4 %copy-start.22 = (pred[2,128]{1,0:T(4,128)(4,1)S(1)}, pred[2,128]{1,0:T(4,128)(4,1)}, u32[]{:S(2)}) copy-start(pred[2,128]{1,0:T(4,128)(4,1)} %fusion.30) | copy-start | bytes 772
  555.0 20.2 %copy-start.16 = (f32[256]{0:T(256)S(1)}, f32[256]{0:T(256)}, u32[]{:S(2)}) copy-start(f32[256]{0:T(256)} %copy-done.15) | copy-start | bytes 3076
  578.4 2.4 copy-start.18
  578.4 2.4 copy-start.20
Sparse Core Ops, SparseCore 0:
  9.6 39.7 all-gather.4
  51.9 230.7 all-gather.2
  286.3 285.8 reduce-scatter.4
  593.0 35.6 reduce-scatter.2
where the time goes:
time: 642 us; the launch traced here: 635 us
  local copies, waits for them, and re-layouts  283 us (44%)
  waiting for transfers between devices  236 us (37%)
  matrix products  71.1 us (11%)
  other arithmetic  17 us (3%)
  between operations  14.3 us (2%)
  blocking collectives  12.9 us (2%)
    all_gather x1, waiting for transfers between devices, local(): piece = lax.all_gather(w_down, 'fsdp', axis=0, tiled=True)  200 us
    gather x48, local copies, waits for them, and re-layouts  109 us
    unnamed x73, local copies, waits for them, and re-layouts  98.7 us
    gather x1, local copies, waits for them, and re-layouts, local(): chosen = jnp.take(piece, safe_exp, axis=1)  41.5 us
    dot_general x1, matrix products, local(): jnp.einsum('bri,dbi->brd', hid_blocks, chosen, preferred_element_type=jnp...  25.9 us
    all_gather x1, waiting for transfers between devices, local(): full_grads = lax.all_gather(grad_out, 'ep', axis=1, tiled=True)  25.9 us
    dot_general x1, matrix products, local(): jnp.einsum('rd,rei->dei', scaled, masked_hid, preferred_element_type=jnp....  24.9 us
    dot_general x1, matrix products, local(): jnp.einsum('brd,dbi->bri', routed_blocks, chosen, preferred_element_type=...  20.2 us
  transfers between devices with their start and end apart: 4, of which 3 were waited for; matrix products, arithmetic and copies ran while one was open for 56% of the time, Pallas kernels for 0%

commit v1 on v0

--- a/solution.py
+++ b/solution.py
@@ -4,6 +4,14 @@
 from jax.sharding import PartitionSpec as P
 
 BLOCK = 128
+
+
+def views_treat(view, dim_at):
+    view = jnp.moveaxis(view, 0, dim_at)
+    seen_now = view.shape
+    return view.reshape(
+        *seen_now[:dim_at], seen_now[dim_at] * seen_now[dim_at + 1], *seen_now[dim_at + 2 :]
+    )
 
 
 def route_layout(route_part, prob_part, expert_count, block_rows, row_count):
@@ -35,6 +43,28 @@
 
 
 def local(hidden, w_down, route_ids, probs, grad_out):
+
+    def _extend_sites(matrix, axis_id, join_dim=0):
+        n_all = lax.axis_size(axis_id)
+        local_next = range(n_all)
+        piece_next = map(lambda h: (h, (h + 1) % n_all), local_next)
+        table = list(piece_next)
+        t_next, built = ([], [])
+        rack = [(w, ii) for ii, w in table]
+        for pp in range(n_all - 1):
+            if pp % 2 == 0:
+                parts_out = lax.ppermute(t_next[-1] if t_next else matrix, axis_id, table)
+                t_next.append(parts_out)
+            else:
+                r2 = lax.ppermute(built[-1] if built else matrix, axis_id, rack)
+                built.append(r2)
+        before = jnp.stack([*t_next[::-1], matrix, *built], axis=0)
+        step_out = lax.axis_index(axis_id)
+        val2 = len(t_next)
+        block_last = step_out - val2
+        before = before[(jnp.arange(n_all) - block_last) % n_all]
+        return views_treat(before, join_dim)
+
     row_count, unit_count = hidden.shape
     expert_count = w_down.shape[1]
     block_count = row_count // BLOCK
@@ -54,7 +84,7 @@
         jnp.bfloat16
     )
     masked_hid = hidden[:, None, :] * member[:, :, None]
-    piece = lax.all_gather(w_down, "fsdp", axis=0, tiled=True)
+    piece = _extend_sites(w_down, "fsdp")
     width = piece.shape[0]
     chosen = jnp.take(piece, safe_exp, axis=1)
     out_rows = jnp.einsum(

time: 642 us -> 1320 us (2.06)
  waiting for transfers between devices: 236 us -> 623 us
  local copies, waits for them, and re-layouts: 283 us -> 516 us
  other arithmetic: 17 us -> 71.1 us
    ppermute x0 -> x7, waiting for transfers between devices: none -> 579 us  [the longest x4 395 us: _extend_sites(): parts_out = lax.ppermute(t_next[-1] if t_next else matrix, axis_id, table)]
    all_gather x1 -> x0, waiting for transfers between devices: 200 us -> none  [local(): piece = lax.all_gather(w_down, 'fsdp', axis=0, tiled=True)]
    gather x48 -> x53, local copies, waits for them, and re-layouts: 109 us -> 277 us  [the longest x5 171 us: _extend_sites(): before = before[(jnp.arange(n_all) - block_last) % n_all]]
    unnamed x73 -> x84, local copies, waits for them, and re-layouts: 98.7 us -> 168 us
    unnamed x0 -> x2, other arithmetic: none -> 51.7 us
  transfers between devices with their start and end apart: 4 -> 10, of which waited for: 3 -> 8; matrix products, arithmetic and copies ran while one was open for 56% -> 49% of each run, Pallas kernels for 0% -> 0%
where the time goes in v1:
time: 1320 us; the launch traced here: 1310 us
  waiting for transfers between devices  623 us (47%)
  local copies, waits for them, and re-layouts  516 us (39%)
  other arithmetic  71.1 us (5%)
  matrix products  66.2 us (5%)
  between operations  14.5 us (1%)
  blocking collectives  14.2 us (1%)
    ppermute x4, waiting for transfers between devices, _extend_sites(): parts_out = lax.ppermute(t_next[-1] if t_next else matrix, axis_id, table)  395 us
    ppermute x3, waiting for transfers between devices, _extend_sites(): r2 = lax.ppermute(built[-1] if built else matrix, axis_id, rack)  184 us
    gather x5, local copies, waits for them, and re-layouts, _extend_sites(): before = before[(jnp.arange(n_all) - block_last) % n_all]  171 us
    unnamed x84, local copies, waits for them, and re-layouts  168 us
    gather x48, local copies, waits for them, and re-layouts  105 us
    unnamed x2, other arithmetic  51.7 us
    gather x1, local copies, waits for them, and re-layouts, local(): chosen = jnp.take(piece, safe_exp, axis=1)  33.2 us
    all_gather x1, waiting for transfers between devices, local(): full_grads = lax.all_gather(grad_out, 'ep', axis=1, tiled=True)  32.9 us
  transfers between devices with their start and end apart: 10, of which 8 were waited for; matrix products, arithmetic and copies ran while one was open for 49% of the time, Pallas kernels for 0%

profile of v1, /device:TPU:0, one launch (start us, length us, event | category | flops | bytes accessed | tf_op | source)
XLA Modules:
  0.0 1314.8 jit_solution(17388387631375160824)
XLA Ops:
  16.5 32.9 %all-gather.2.cloned.1.call-done = bf16[128,6144]{1,0:T(8,128)(2,1)} async-done(((bf16[128,1536]{1,0:T(8,128)(2,1)}), bf16[128,6144]{1,0:T(8,128)(2,1)}) %all-gather.2.cloned.1.call-update) | async-done | bytes 1572880 | tf_op jit(solution)/shard_map/all_gather | solution.py:76
  49.4 7.1 gather_fusion.1
  56.5 23.1 %collective-permute-done = bf16[768,2,2048]{2,1,0:T(2,128)(2,1)} collective-permute-done((bf16[768,2,2048]{2,1,0:T(2,128)(2,1)}, bf16[768,2,2048]{2,1,0:T(2,128)(2,1)}, u32[]{:S(2)}, u32[]{:S(2)}) %collective-permute-start) | collective-permute-done | bytes 6291488 | tf_op jit(solution)/shard_map/ppermute | solution.py:56
  79.8 21.7 %convolution_convert_fusion = bf16[6144,2,2048]{2,0,1:T(8,128)(2,1)} fusion(bf16[256,6144]{1,0:T(8,128)(2,1)S(1)} %gather_fusion.1, f32[256]{0:T(256)S(1)} %scatter_custom_fusion, pred[256]{0:T(512)(128)(4,1)S(1)} %broadcast_compare_fusion, bf16[256,2]{0,1:T(2,128)(2,1)S(1)} %compare_convert_fusion, bf16[256,2048]{1,0:T(8,128)(2,1)} %param.5), kind=kOutput, calls=%fused_computation.36 | convolution fusion | flops 12920553472 | bytes 54528256 | tf_op jit(solution)/shard_map/rd,rei->dei/dot_general | solution.py:100
  104.3 105.6 %collective-permute-done.1 = bf16[768,2,2048]{2,1,0:T(2,128)(2,1)} collective-permute-done((bf16[768,2,2048]{2,1,0:T(2,128)(2,1)}, bf16[768,2,2048]{2,1,0:T(2,128)(2,1)}, u32[]{:S(2)}, u32[]{:S(2)}) %collective-permute-start.1) | collective-permute-done | bytes 6291488 | tf_op jit(solution)/shard_map/ppermute | solution.py:56
  209.9 92.6 %collective-permute-done.4 = bf16[768,2,2048]{2,1,0:T(2,128)(2,1)} collective-permute-done((bf16[768,2,2048]{2,1,0:T(2,128)(2,1)}, bf16[768,2,2048]{2,1,0:T(2,128)(2,1)}, u32[]{:S(2)}, u32[]{:S(2)}) %collective-permute-start.4) | collective-permute-done | bytes 6291488 | tf_op jit(solution)/shard_map/ppermute | solution.py:59
  305.3 167.9 %collective-permute-done.2 = bf16[768,2,2048]{2,1,0:T(2,128)(2,1)} collective-permute-done((bf16[768,2,2048]{2,1,0:T(2,128)(2,1)}, bf16[768,2,2048]{2,1,0:T(2,128)(2,1)}, u32[]{:S(2)}, u32[]{:S(2)}) %collective-permute-start.2) | collective-permute-done | bytes 6291488 | tf_op jit(solution)/shard_map/ppermute | solution.py:56
  475.1 90.9 %collective-permute-done.5 = bf16[768,2,2048]{2,1,0:T(2,128)(2,1)} collective-permute-done((bf16[768,2,2048]{2,1,0:T(2,128)(2,1)}, bf16[768,2,2048]{2,1,0:T(2,128)(2,1)}, u32[]{:S(2)}, u32[]{:S(2)}) %collective-permute-start.5) | collective-permute-done | bytes 6291488 | tf_op jit(solution)/shard_map/ppermute | solution.py:59
  568.9 98.7 %collective-permute-done.3 = bf16[768,2,2048]{2,1,0:T(2,128)(2,1)} collective-permute-done((bf16[768,2,2048]{2,1,0:T(2,128)(2,1)}, bf16[768,2,2048]{2,1,0:T(2,128)(2,1)}, u32[]{:S(2)}, u32[]{:S(2)}) %collective-permute-start.3) | collective-permute-done | bytes 6291488 | tf_op jit(solution)/shard_map/ppermute | solution.py:56
  667.5 6.7 bitcast_dynamic-update-slice_fusion.19
  674.2 6.7 bitcast_dynamic-update-slice_fusion.18
  681.0 7.3 bitcast_dynamic-update-slice_fusion.17
  688.3 6.9 bitcast_dynamic-update-slice_fusion.16
  695.2 5.4 bitcast_dynamic-update-slice_fusion.15
  700.6 6.7 bitcast_dynamic-update-slice_fusion.14
  707.3 6.7 bitcast_dynamic-update-slice_fusion.13
  714.1 5.4 bitcast_dynamic-update-slice_fusion.12
  719.5 38.3 %fusion.31 = (bf16[8,768,2,512]{3,2,1,0:T(2,128)(2,1)}, bf16[8,768,2,512]{3,2,1,0:T(2,128)(2,1)}, bf16[8,768,2,512]{3,2,1,0:T(2,128)(2,1)}, bf16[8,768,2,512]{3,2,1,0:T(2,128)(2,1)}) fusion(bf16[8,768,2,2048]{3,2,1,0:T(2,128)(2,1)} %bitcast_dynamic-update-slice_fusion.12), kind=kLoop, calls=%fused_computation.129 | loop fusion | bytes 100663296 | tf_op jit(solution)/shard_map/gather | solution.py:65
  757.8 31.0 %gather_fusion.3 = bf16[8,768,2,512]{3,2,1,0:T(2,128)(2,1)} fusion(bf16[8,768,2,512]{3,2,1,0:T(2,128)(2,1)} %get-tuple-element.223, s32[1024]{0:T(1024)S(1)} %get-tuple-element.234), kind=kCustom, calls=%fused_computation.3 | custom fusion | bytes 25165856 | tf_op jit(solution)/shard_map/gather | solution.py:65
  788.8 31.0 %gather_fusion.4 = bf16[8,768,2,512]{3,2,1,0:T(2,128)(2,1)} fusion(bf16[8,768,2,512]{3,2,1,0:T(2,128)(2,1)} %get-tuple-element.225, s32[1024]{0:T(1024)S(1)} %get-tuple-element.234), kind=kCustom, calls=%fused_computation.4 | custom fusion | bytes 25165856 | tf_op jit(solution)/shard_map/gather | solution.py:65
  819.8 39.7 %gather_fusion.5 = bf16[8,768,2,512]{3,2,1,0:T(2,128)(2,1)} fusion(bf16[8,768,2,512]{3,2,1,0:T(2,128)(2,1)} %get-tuple-element.224, s32[1024]{0:T(1024)S(1)} %get-tuple-element.234), kind=kCustom, calls=%fused_computation.5 | custom fusion | bytes 25165856 | tf_op jit(solution)/shard_map/gather | solution.py:65
  859.6 31.0 %gather_fusion.6 = bf16[8,768,2,512]{3,2,1,0:T(2,128)(2,1)} fusion(bf16[8,768,2,512]{3,2,1,0:T(2,128)(2,1)} %get-tuple-element.226, s32[1024]{0:T(1024)S(1)} %get-tuple-element.234), kind=kCustom, calls=%fused_computation.6 | custom fusion | bytes 25165856 | tf_op jit(solution)/shard_map/gather | solution.py:65
  890.6 51.7 %pad_maximum_fusion = bf16[8,768,2,2048]{3,2,1,0:T(2,128)(2,1)} fusion(bf16[8,768,2,512]{3,2,1,0:T(2,128)(2,1)} %gather_fusion.6, bf16[8,768,2,512]{3,2,1,0:T(2,128)(2,1)} %gather_fusion.5, bf16[8,768,2,512]{3,2,1,0:T(2,128)(2,1)} %gather_fusion.4, bf16[8,768,2,512]{3,2,1,0:T(2,128)(2,1)} %gather_fusion.3), kind=kLoop, calls=%fused_computation.34 | loop fusion | flops 201326592 | bytes 100663296
  942.3 33.4 %copy.21 = bf16[8,768,2,2048]{3,1,0,2:T(8,128)(2,1)} copy(bf16[8,768,2,2048]{3,2,1,0:T(2,128)(2,1)} %pad_maximum_fusion) | data formatting | bytes 100663296
  975.7 33.2 %fusion.30 = (bf16[512,2,2048]{2,0,1:T(8,128)(2,1)}, bf16[512,2,2048]{2,0,1:T(8,128)(2,1)}, bf16[512,2,2048]{2,0,1:T(8,128)(2,1)}, bf16[512,2,2048]{2,0,1:T(8,12...) fusion(bf16[6144,2,2048]{2,0,1:T(8,128)(2,1)} %bitcast.167), kind=kLoop, calls=%fused_computation.128 | loop fusion | bytes 100663296 | tf_op jit(solution)/shard_map/jit(_take)/gather | solution.py:89
  1011.3 8.5 while.12
  1022.4 8.9 while.13
  1033.7 8.8 while.14
  1045.1 8.8 while.15
  1056.3 9.0 while.16
  1067.8 8.8 while.17
  1079.2 8.8 while.18
  1084.1 3.9 bitcast_dynamic-update-slice_fusion.50
  1090.5 8.7 while.19
  1101.8 8.8 while.20
  1113.0 8.8 while.21
  1124.5 8.8 while.22
  1129.4 3.9 bitcast_dynamic-update-slice_fusion.54
  1135.8 8.8 while.23
  1144.6 4.9 bitcast_dynamic-update-slice_fusion.31
  1188.8 25.0 %fusion.1 = f32[2,6144,128]{1,2,0:T(8,128)} fusion(bf16[2,128,2048]{2,1,0:T(8,128)(2,1)S(1)} %bitcast.169, bf16[6144,2,2048]{2,0,1:T(8,128)(2,1)} %bitcast_dynamic-update-slice_fusion.20, pred[2]{0:T(512)(128)(4,1)S(1)} %copy-done.22), kind=kOutput, calls=%fused_computation.38 | convolution fusion | flops 6467616768 | bytes 57671680 | tf_op jit(solution)/shard_map/bri,dbi->brd/dot_general | solution.py:90
  1213.8 10.6 gather_fusion
  1224.4 8.3 reshape.558
  1232.7 19.5 %fusion = f32[2,128,2048]{2,1,0:T(8,128)} fusion(bf16[6144,2,2048]{2,0,1:T(8,128)(2,1)} %bitcast_dynamic-update-slice_fusion.20, pred[2]{0:T(512)(128)(4,1)S(1)} %copy-done.22, bf16[2,128,6144]{2,1,0:T(8,128)(2,1)S(1)} %bitcast.168, pred[2,128]{1,0:T(4,128)(4,1)S(1)} %copy-done.21), kind=kOutput, calls=%fused_computation.37 | convolution fusion | flops 6469189632 | bytes 55574784 | tf_op jit(solution)/shard_map/brd,dbi->bri/dot_general | solution.py:93
  1257.6 11.9 multiply_reduce_fusion
  1269.5 14.2 %psum.7 = f32[128,2]{0,1:T(2,128)} all-reduce(f32[128,2]{0,1:T(2,128)S(1)} %get-tuple-element.229), channel_id=1, replica_groups=mesh['fsdp'=8,'ep'=4] {'ep'}, use_global_device_ids=true, to_apply=%region_14.15 | all-reduce | flops 256 | bytes 2048 | tf_op jit(solution)/shard_map/psum | solution.py:112
  1283.7 12.6 copy.30
  1296.3 11.5 reduce-scatter.3.cloned.1.call-done
  (177 shorter events, 192.1 us)
Async XLA Ops:
  7.2 42.2 %all-gather.2.cloned.1.call-start = ((), (), s32[]{:S(2)}) async-start(), calls=%async_computation.3 | async-start | bytes 1966080 | tf_op jit(solution)/shard_map/all_gather | solution.py:76
  7.2 72.4 %collective-permute-start = (bf16[768,2,2048]{2,1,0:T(2,128)(2,1)}, bf16[768,2,2048]{2,1,0:T(2,128)(2,1)}, u32[]{:S(2)}, u32[]{:S(2)}) collective-permute-start(bf16[768,2,2048]{2,1,0:T(2,128)(2,1)} %param.6), channel_id=1, source_target_pairs={{0,4},{4,8},{8,12},{12,16},{16,20},{20,24},{24,28},{28,0},{1,5},{5... | collective-permute-start | bytes 18874376 | tf_op jit(solution)/shard_map/ppermute | solution.py:56
  7.9 1275.8 %reduce-scatter.5.cloned.1.call-start = ((), (), s32[]{:S(2)}) async-start(), calls=%async_computation.4 | async-start | bytes 56623104 | tf_op jit(solution)/shard_map/reduce_scatter | solution.py:99
  8.8 7.8 copy-start.17
  15.6 64.2 %copy-start.15 = (f32[256]{0:T(256)}, f32[256]{0:T(256)S(1)}, u32[]{:S(2)}) copy-start(f32[256]{0:T(256)S(1)} %scatter_custom_fusion) | copy-start | bytes 3076
  56.5 45.1 %copy-start.11 = (bf16[256,6144]{1,0:T(8,128)(2,1)}, bf16[256,6144]{1,0:T(8,128)(2,1)S(1)}, u32[]{:S(2)}) copy-start(bf16[256,6144]{1,0:T(8,128)(2,1)S(1)} %gather_fusion.1) | copy-start | bytes 9437188
  79.6 130.3 %collective-permute-start.1 = (bf16[768,2,2048]{2,1,0:T(2,128)(2,1)}, bf16[768,2,2048]{2,1,0:T(2,128)(2,1)}, u32[]{:S(2)}, u32[]{:S(2)}) collective-permute-start(bf16[768,2,2048]{2,1,0:T(2,128)(2,1)} %collective-permute-done), channel_id=1, source_target_pairs={{0,4},{4,8},{8,12},{12,16},{16,20},{20,24},{24,28},{28,0},{1,5},{5... | collective-permute-start | bytes 18874376 | tf_op jit(solution)/shard_map/ppermute | solution.py:56
  101.6 1206.3 %reduce-scatter.3.cloned.1.call-start = ((), (), s32[]{:S(2)}) async-start(), calls=%async_computation.2 | async-start | bytes 1966080 | tf_op jit(solution)/shard_map/reduce_scatter | solution.py:107
  101.6 200.9 %collective-permute-start.4 = (bf16[768,2,2048]{2,1,0:T(2,128)(2,1)}, bf16[768,2,2048]{2,1,0:T(2,128)(2,1)}, u32[]{:S(2)}, u32[]{:S(2)}) collective-permute-start(bf16[768,2,2048]{2,1,0:T(2,128)(2,1)} %param.6), channel_id=1, source_target_pairs={{4,0},{8,4},{12,8},{16,12},{20,16},{24,20},{28,24},{0,28},{5,1},{9... | collective-permute-start | bytes 18874376 | tf_op jit(solution)/shard_map/ppermute | solution.py:59
  209.9 263.3 %collective-permute-start.2 = (bf16[768,2,2048]{2,1,0:T(2,128)(2,1)}, bf16[768,2,2048]{2,1,0:T(2,128)(2,1)}, u32[]{:S(2)}, u32[]{:S(2)}) collective-permute-start(bf16[768,2,2048]{2,1,0:T(2,128)(2,1)} %collective-permute-done.1), channel_id=1, source_target_pairs={{0,4},{4,8},{8,12},{12,16},{16,20},{20,24},{24,28},{28,0},{1,5},{5... | collective-permute-start | bytes 18874376 | tf_op jit(solution)/shard_map/ppermute | solution.py:56
  302.5 263.5 %collective-permute-start.5 = (bf16[768,2,2048]{2,1,0:T(2,128)(2,1)}, bf16[768,2,2048]{2,1,0:T(2,128)(2,1)}, u32[]{:S(2)}, u32[]{:S(2)}) collective-permute-start(bf16[768,2,2048]{2,1,0:T(2,128)(2,1)} %collective-permute-done.4), channel_id=1, source_target_pairs={{4,0},{8,4},{12,8},{16,12},{20,16},{24,20},{28,24},{0,28},{5,1},{9... | collective-permute-start | bytes 18874376 | tf_op jit(solution)/shard_map/ppermute | solution.py:59
  473.2 194.3 %collective-permute-start.3 = (bf16[768,2,2048]{2,1,0:T(2,128)(2,1)}, bf16[768,2,2048]{2,1,0:T(2,128)(2,1)}, u32[]{:S(2)}, u32[]{:S(2)}) collective-permute-start(bf16[768,2,2048]{2,1,0:T(2,128)(2,1)} %collective-permute-done.2), channel_id=1, source_target_pairs={{0,4},{4,8},{8,12},{12,16},{16,20},{20,24},{24,28},{28,0},{1,5},{5... | collective-permute-start | bytes 18874376 | tf_op jit(solution)/shard_map/ppermute | solution.py:56
  566.1 148.0 %collective-permute-start.6 = (bf16[768,2,2048]{2,1,0:T(2,128)(2,1)}, bf16[768,2,2048]{2,1,0:T(2,128)(2,1)S(1)}, u32[]{:S(2)}, u32[]{:S(2)}) collective-permute-start(bf16[768,2,2048]{2,1,0:T(2,128)(2,1)} %collective-permute-done.5), channel_id=1, source_target_pairs={{4,0},{8,4},{12,8},{16,12},{20,16},{24,20},{28,24},{0,28},{5,1},{9... | collective-permute-start | bytes 18874376 | tf_op jit(solution)/shard_map/ppermute | solution.py:59
  681.0 14.2 %slice-start = ((s8[6291456]{0:T(1024)(128)(4,1)}), s8[4194304]{0:T(1024)(128)(4,1)S(1)}, s32[]{:S(2)}) async-start(s8[6291456]{0:T(1024)(128)(4,1)} %bitcast.170), calls=%async_computation.5 | async-start | bytes 8388608
  688.3 6.9 slice-start.1
  1008.9 2.5 copy-start.20
  1144.6 4.9 copy-start.1
  1149.5 3.7 copy-start.2
  1153.2 3.7 copy-start.3
  1156.9 3.7 copy-start.4
  1160.6 3.7 copy-start.5
  1164.3 3.7 copy-start.6
  1168.0 3.7 copy-start.7
  1171.7 3.7 copy-start.8
  1175.4 3.7 copy-start.9
  1179.1 3.7 copy-start.10
  1182.8 3.7 copy-start
  1186.5 2.3 copy-start.13
  1186.5 2.3 copy-start.22
  1188.8 25.1 %copy-start.14 = (s32[1024]{0:T(1024)S(1)}, s32[1024]{0:T(1024)}, u32[]{:S(2)}) copy-start(s32[1024]{0:T(1024)} %get-tuple-element.233) | copy-start | bytes 12292
  1224.4 8.3 copy-start.12
  1224.4 8.3 copy-start.21
  1232.7 19.5 %copy-start.16 = (f32[256]{0:T(256)S(1)}, f32[256]{0:T(256)}, u32[]{:S(2)}) copy-start(f32[256]{0:T(256)} %copy-done.15) | copy-start | bytes 3076
  1255.3 2.2 copy-start.18
  1255.3 2.2 copy-start.19
Sparse Core Ops, SparseCore 0:
  9.6 39.7 all-gather.1
  101.7 488.1 reduce-scatter.4
  1269.7 38.1 reduce-scatter.2
